TPU v7x, 32 devices: a whole 2x2x4 slice. The times are simulated.
32 devices in a mesh: dp: 2 (over y), expert: 16 (over z, x, core).
Axes of the slice: x: 2, y: 2, z: 4, core: 2. Of those that a mesh axis runs over, the one named last changes fastest.
Arguments:
- soft_tokens: bfloat16 [2048, 2048], P('expert', 'dp'), may hold values from -6 to 6
- expert_ids: int32 [2048, 8], P('expert'), may hold values from 0 to 31, all different within a row; in each aligned block of 128 rows (0 to 127, 128 to 255, ...) at most 40 rows name the same one
- gate_mix: float32 [2048, 8], P('expert'), may hold values from 0.05 to 0.35
- w_gate: bfloat16 [32, 2048, 768], P('expert', 'dp'), may hold values from -0.125 to 0.125
- w_up: bfloat16 [32, 2048, 768], P('expert', 'dp'), may hold values from -0.125 to 0.125
- w_down: bfloat16 [32, 768, 2048], P('expert', None, 'dp'), may hold values from -0.21875 to 0.21875
- out_grad: bfloat16 [2048, 2048], P('expert', 'dp'), may hold values from -6 to 6
Outputs:
- mixed: bfloat16 [2048, 2048], P('expert', 'dp')
- token_grad: bfloat16 [2048, 2048], P('expert', 'dp')
Inputs may be any that keep to these rules, and one draw needn't show every extreme that they name: `expert_ids`: each row names 8 different experts. Among the 128 rows of one device no expert is named by more than 40 rows, and in some device one expert is named by exactly 40 rows.
All inputs are finite; a program needn't handle non-finite values.
Results may differ from a plain program's by a relative error of at most 0.023.
Values may be sent and summed in bfloat16 or wider, within the bound.
A program may use at most 128 MiB of HBM per device.

v0:
```python
import jax
import jax.numpy as jnp
from jax import lax
from jax.sharding import PartitionSpec as P


def slot_table(expert_ids, experts, capacity):
    tok_rows, top_count = expert_ids.shape
    flat_count = tok_rows * top_count
    flat_ids = expert_ids.reshape(flat_count)
    onehot = (flat_ids[:, None] == jnp.arange(experts, dtype=jnp.int32)[None, :]).astype(jnp.int32)
    before = jnp.sum(jnp.cumsum(onehot, axis=0) * onehot, axis=1) - 1
    position = flat_ids * capacity + before
    source = jnp.full((experts * capacity,), flat_count, jnp.int32)
    source = source.at[position].set(jnp.arange(flat_count, dtype=jnp.int32))
    return (position, source)


def place_rows(values, source, top_count):
    tok_rows = values.shape[0]
    valid = source < tok_rows * top_count
    token = jnp.minimum(source // top_count, tok_rows - 1)
    return jnp.where(valid[:, None], values[token], jnp.zeros((), values.dtype))


def activate(sums, hidden):
    gate_part = sums[..., :hidden]
    upper_part = sums[..., hidden:]
    sigmoid_gate = jax.nn.sigmoid(gate_part)
    return (gate_part * sigmoid_gate * upper_part).astype(jnp.bfloat16)


def act_grad(sums, back, hidden):
    gate_part = sums[..., :hidden]
    upper_part = sums[..., hidden:]
    sigmoid_gate = jax.nn.sigmoid(gate_part)
    d_gate = back * upper_part * sigmoid_gate * (1.0 + gate_part * (1.0 - sigmoid_gate))
    d_upper = back * gate_part * sigmoid_gate
    return jnp.concatenate([d_gate, d_upper], axis=-1).astype(jnp.bfloat16)


def combine(returned, position, gate_mix):
    tok_rows, top_count = gate_mix.shape
    flat_rows = returned.reshape(-1, returned.shape[-1])
    picked = flat_rows[position].reshape(tok_rows, top_count, -1).astype(jnp.float32)
    return jnp.sum(gate_mix[:, :, None] * picked, axis=1).astype(jnp.bfloat16)


def per_device(soft_tokens, expert_ids, gate_mix, w_gate, w_up, w_down, out_grad):
    tok_rows, width_part = soft_tokens.shape
    top_count = expert_ids.shape[1]
    local_experts = w_gate.shape[0]
    hidden = w_gate.shape[2]
    groups = lax.axis_size("expert")
    experts = groups * local_experts
    capacity = max(2, tok_rows * top_count * 5 // (4 * experts))
    position, source = slot_table(expert_ids, experts, capacity)
    w_both = jnp.concatenate([w_gate, w_up], axis=2)
    layout = (groups, local_experts, capacity, width_part)
    token_rows = place_rows(soft_tokens, source, top_count).reshape(layout)
    grad_rows_out = place_rows(out_grad, source, top_count).reshape(layout)
    token_recv = lax.all_to_all(token_rows, "expert", split_axis=0, concat_axis=0, tiled=True)
    dp_count = lax.axis_size("dp")
    share = groups // dp_count
    first_row = lax.axis_index("dp") * share
    piece = token_recv
    own_sums = lax.psum_scatter(
        jnp.einsum("secd,edf->secf", piece, w_both, preferred_element_type=jnp.float32).astype(
            jnp.bfloat16
        ),
        "dp",
        scatter_dimension=0,
        tiled=True,
    ).astype(jnp.float32)
    hidden_act = lax.all_gather(activate(own_sums, hidden), "dp", axis=0, tiled=True)
    expert_out = jnp.einsum(
        "secf,efd->secd", hidden_act, w_down, preferred_element_type=jnp.float32
    ).astype(jnp.bfloat16)
    out_returned = lax.all_to_all(expert_out, "expert", split_axis=0, concat_axis=0, tiled=True)
    grad_recv = lax.all_to_all(grad_rows_out, "expert", split_axis=0, concat_axis=0, tiled=True)
    piece = grad_recv
    whole_back = lax.psum(
        jnp.einsum("secd,efd->secf", piece, w_down, preferred_element_type=jnp.float32).astype(
            jnp.bfloat16
        ),
        "dp",
    ).astype(jnp.float32)
    own_back = lax.dynamic_slice_in_dim(whole_back, first_row, share, 0)
    dpre = lax.all_gather(act_grad(own_sums, own_back, hidden), "dp", axis=0, tiled=True)
    grad_rows = jnp.einsum(
        "secf,edf->secd", dpre, w_both, preferred_element_type=jnp.float32
    ).astype(jnp.bfloat16)
    grad_returned = lax.all_to_all(grad_rows, "expert", split_axis=0, concat_axis=0, tiled=True)
    mixed = combine(out_returned, position, gate_mix)
    token_grad = combine(grad_returned, position, gate_mix)
    return (mixed, token_grad)


def solution(mesh):
    in_specs = (
        P("expert", "dp"),
        P("expert", None),
        P("expert", None),
        P("expert", "dp", None),
        P("expert", "dp", None),
        P("expert", None, "dp"),
        P("expert", "dp"),
    )
    out_specs = (P("expert", "dp"), P("expert", "dp"))
    return jax.shard_map(
        per_device, mesh=mesh, in_specs=in_specs, out_specs=out_specs, check_vma=False
    )
```

profile of v0, /device:TPU:11, one launch (start us, length us, event | category | flops | bytes accessed | tf_op | source)
XLA Modules:
  0.0 453.7 jit_solution(9259662578411656731)
XLA Ops:
  7.2 1.0 copy.23
  9.0 1.3 broadcast_multiply_fusion
  10.9 15.7 %reduce-window.6 = s32[32,8,128]{2,1,0:T(8,128)S(1)} reduce-window(s32[32,8,128]{2,1,0:T(8,128)} %fusion.23, s32[]{:T(128)} %constant.19.clone.1), window={size=1x1x128 pad=0_0x0_0x127_0}, to_apply=%region_0.0 | reduce-window | flops 4161536 | bytes 262148 | tf_op jit(solution)/shard_map/reduce-window
  27.4 1.0 copy.25
  31.5 4.3 scatter_custom_fusion
  35.9 5.1 %gather_fusion.2 = bf16[1280,1024]{1,0:T(8,128)(2,1)} fusion(bf16[128,1024]{1,0:T(8,128)(2,1)S(1)} %copy-done.1, s32[2048]{0:T(1024)S(1)} %pad_clamp_fusion), kind=kCustom, calls=%fused_computation.2 | custom fusion | bytes 5248000 | tf_op jit(solution)/shard_map/gather | solution.py:23
  41.0 7.7 %gather_fusion = bf16[1280,1024]{1,0:T(8,128)(2,1)} fusion(bf16[128,1024]{1,0:T(8,128)(2,1)} %param.7, s32[2048]{0:T(1024)S(1)} %pad_clamp_fusion), kind=kCustom, calls=%fused_computation | custom fusion | bytes 5248000 | tf_op jit(solution)/shard_map/gather | solution.py:23
  48.8 3.9 broadcast_select_fusion
  52.7 64.9 %all_to_all.20 = bf16[16,2,40,1024]{3,2,1,0:T(8,128)(2,1)} all-to-all(bf16[16,2,40,1024]{3,2,1,0:T(8,128)(2,1)S(1)} %get-tuple-element.8), channel_id=1, replica_groups=mesh['dp'=2,'expert'=16] {'expert'}, dimensions={0} | all-to-all | bytes 5242880 | tf_op jit(solution)/shard_map/all_to_all | solution.py:62
  117.6 9.7 %fusion.3 = bf16[16,2,40,1536]{3,2,0,1:T(8,128)(2,1)} fusion(bf16[2,1024,768]{2,1,0:T(8,128)(2,1)} %param.11, bf16[2,1024,768]{2,1,0:T(8,128)(2,1)} %param.10, bf16[16,2,40,1024]{3,2,1,0:T(8,128)(2,1)} %all_to_all.20), kind=kOutput, calls=%fused_computation.12 | convolution fusion | flops 4041080832 | bytes 12845056 | tf_op jit(solution)/shard_map/secd,edf->secf/dot_general | solution.py:68
  127.3 2.6 copy.33
  129.9 4.0 copy.36
  134.0 63.6 %all_to_all.21 = bf16[16,2,40,1024]{3,2,1,0:T(8,128)(2,1)S(1)} all-to-all(bf16[16,2,40,1024]{3,2,1,0:T(8,128)(2,1)} %get-tuple-element.7), channel_id=1, replica_groups=mesh['dp'=2,'expert'=16] {'expert'}, dimensions={0} | all-to-all | bytes 5242880 | tf_op jit(solution)/shard_map/all_to_all | solution.py:80
  197.6 3.6 convert_bitcast_fusion.2
  201.3 2.1 copy.37
  203.4 2.4 copy_convert_fusion
  205.8 55.2 %all-reduce.2.cloned.1.call-done = bf16[16,2,40,768]{3,2,0,1:T(8,128)(2,1)} async-done(((bf16[16,2,40,768]{3,2,0,1:T(8,128)(2,1)}), bf16[16,2,40,768]{3,2,0,1:T(8,128)(2,1)}) %all-reduce.2.cloned.1.call-update) | async-done | bytes 1966096 | tf_op jit(solution)/shard_map/psum | solution.py:82
  261.1 5.1 %fusion.16 = (bf16[8,2,40,768]{3,2,0,1:T(8,128)(2,1)}, bf16[8,2,40,768]{3,2,0,1:T(8,128)(2,1)}, bf16[8,2,40,768]{3,2,0,1:T(8,128)(2,1)}) fusion(f32[8,2,40,1536]{3,2,0,1:T(8,128)} %copy_convert_fusion, bf16[16,2,40,768]{3,2,0,1:T(8,128)(2,1)} %all-reduce.2.cloned.1.call-done, s32[]{:T(128)S(6)} %select_n.39), kind=kLoop, calls=%fused_computation.29 | loop fusion | flops 8355840 | bytes 7864324 | tf_op jit(solution)/shard_map/convert.2
  266.3 3.0 pad_maximum_fusion
  269.2 28.7 %all-gather.3.cloned.1.call-done = bf16[16,2,40,768]{3,2,0,1:T(8,128)(2,1)} async-done(((bf16[8,2,40,768]{3,2,0,1:T(8,128)(2,1)}), bf16[16,2,40,768]{3,2,0,1:T(8,128)(2,1)}) %all-gather.3.cloned.1.call-update) | async-done | bytes 1966096 | tf_op jit(solution)/shard_map/all_gather | solution.py:75
  298.0 3.8 convert_bitcast_fusion.1
  301.7 1.8 copy.28
  303.6 6.5 %all-to-all-start.1 = ((bf16[16,2,40,1024]{3,2,1,0:T(8,128)(2,1)}), bf16[16,2,40,1024]{3,2,1,0:T(8,128)(2,1)}, u32[]{:S(2)}, u32[]{:S(2)}) async-start(bf16[16,2,40,1024]{3,2,1,0:T(8,128)(2,1)} %copy.28), calls=%async_computation.1 | async-start | bytes 5242880 | tf_op jit(solution)/shard_map/all_to_all | solution.py:79
  310.1 43.1 %all-gather.5.cloned.1.call-done = bf16[16,2,40,1536]{3,2,0,1:T(8,128)(2,1)} async-done(((bf16[8,2,40,1536]{3,2,0,1:T(8,128)(2,1)}), bf16[16,2,40,1536]{3,2,0,1:T(8,128)(2,1)}) %all-gather.5.cloned.1.call-update) | async-done | bytes 3932176 | tf_op jit(solution)/shard_map/all_gather | solution.py:89
  353.2 8.3 %convert_bitcast_fusion = bf16[16,2,40,1024]{3,2,0,1:T(8,128)(2,1)S(1)} fusion(bf16[16,2,40,1536]{3,2,0,1:T(8,128)(2,1)} %all-gather.5.cloned.1.call-done, bf16[2,1024,768]{2,1,0:T(8,128)(2,1)} %param.11, bf16[2,1024,768]{2,1,0:T(8,128)(2,1)} %param.10), kind=kOutput, calls=%fused_computation.19 | convolution fusion | flops 4040425472 | bytes 12845056 | tf_op jit(solution)/shard_map/secf,edf->secd/dot_general | solution.py:90
  361.5 1.8 copy.30
  363.3 5.5 %all-to-all-done.1 = bf16[16,2,40,1024]{3,2,1,0:T(8,128)(2,1)} async-done(((bf16[16,2,40,1024]{3,2,1,0:T(8,128)(2,1)}), bf16[16,2,40,1024]{3,2,1,0:T(8,128)(2,1)}, u32[]{:S(2)}, u32[]{:S(2)}) %all-to-all-start.1) | async-done | bytes 2621472 | tf_op jit(solution)/shard_map/all_to_all | solution.py:79
  368.8 4.8 %all-to-all-start.3 = ((bf16[16,2,40,1024]{3,2,1,0:T(8,128)(2,1)}), bf16[16,2,40,1024]{3,2,1,0:T(8,128)(2,1)}, u32[]{:S(2)}, u32[]{:S(2)}) async-start(bf16[16,2,40,1024]{3,2,1,0:T(8,128)(2,1)} %copy.30), calls=%async_computation.3 | async-start | bytes 5242880 | tf_op jit(solution)/shard_map/all_to_all | solution.py:93
  373.7 8.1 %gather_fusion.1 = bf16[1024,1024]{1,0:T(8,128)(2,1)} fusion(bf16[1280,1024]{1,0:T(8,128)(2,1)} %bitcast.11, s32[1024]{0:T(1024)S(1)} %broadcast_clamp_fusion), kind=kCustom, calls=%fused_computation.1 | custom fusion | bytes 4198400 | tf_op jit(solution)/shard_map/gather | solution.py:45
  381.9 50.5 %all-to-all-done.3 = bf16[16,2,40,1024]{3,2,1,0:T(8,128)(2,1)} async-done(((bf16[16,2,40,1024]{3,2,1,0:T(8,128)(2,1)}), bf16[16,2,40,1024]{3,2,1,0:T(8,128)(2,1)}, u32[]{:S(2)}, u32[]{:S(2)}) %all-to-all-start.3) | async-done | bytes 2621472 | tf_op jit(solution)/shard_map/all_to_all | solution.py:93
  432.4 8.1 %gather_fusion.3 = bf16[1024,1024]{1,0:T(8,128)(2,1)} fusion(bf16[1280,1024]{1,0:T(8,128)(2,1)} %bitcast.18, s32[1024]{0:T(1024)S(1)} %broadcast_clamp_fusion), kind=kCustom, calls=%fused_computation.3 | custom fusion | bytes 4198400 | tf_op jit(solution)/shard_map/gather | solution.py:45
  440.5 6.7 %fusion = (bf16[128,1024]{1,0:T(8,128)(2,1)}, bf16[128,1024]{1,0:T(8,128)(2,1)}) fusion(bf16[1024,1024]{1,0:T(8,128)(2,1)} %gather_fusion.3, f32[128,8]{1,0:T(8,128)S(1)} %copy.21, bf16[1024,1024]{1,0:T(8,128)(2,1)} %gather_fusion.1), kind=kLoop, calls=%fused_computation.7 | loop fusion | flops 6029312 | bytes 4722688 | tf_op jit(solution)/shard_map/reduce_sum | solution.py:46
  (35 shorter events, 5.8 us)
Async XLA Ops:
  7.2 190.4 %copy-start = (bf16[2,768,1024]{2,1,0:T(8,128)(2,1)S(1)}, bf16[2,768,1024]{2,1,0:T(8,128)(2,1)}, u32[]{:S(2)}) copy-start(bf16[2,768,1024]{2,1,0:T(8,128)(2,1)} %param.12) | copy-start | bytes 9437188
  7.2 28.7 %copy-start.1 = (bf16[128,1024]{1,0:T(8,128)(2,1)S(1)}, bf16[128,1024]{1,0:T(8,128)(2,1)}, u32[]{:S(2)}) copy-start(bf16[128,1024]{1,0:T(8,128)(2,1)} %param.13) | copy-start | bytes 786436
  7.2 194.1 %reduce-scatter.5.cloned.1.call-start = ((), (), s32[]{:S(2)}) async-start(), calls=%async_computation.8 | async-start | bytes 5898240
  134.0 127.1 %all-reduce.2.cloned.1.call-start = ((), (), s32[]{:S(2)}) async-start(), calls=%async_computation.6 | async-start | bytes 3932160 | tf_op jit(solution)/shard_map/psum | solution.py:82
  201.2 96.7 %all-gather.3.cloned.1.call-start = ((), (), s32[]{:S(2)}) async-start(), calls=%async_computation.5 | async-start | bytes 2949120 | tf_op jit(solution)/shard_map/all_gather | solution.py:75
  266.2 87.0 %all-gather.5.cloned.1.call-start = ((), (), s32[]{:S(2)}) async-start(), calls=%async_computation.7 | async-start | bytes 5898240 | tf_op jit(solution)/shard_map/all_gather | solution.py:89
  303.6 65.3 %all-to-all-start.1 = ((bf16[16,2,40,1024]{3,2,1,0:T(8,128)(2,1)}), bf16[16,2,40,1024]{3,2,1,0:T(8,128)(2,1)}, u32[]{:S(2)}, u32[]{:S(2)}) async-start(bf16[16,2,40,1024]{3,2,1,0:T(8,128)(2,1)} %copy.28), calls=%async_computation.1 | async-start | bytes 5242880 | tf_op jit(solution)/shard_map/all_to_all | solution.py:79
  363.3 10.3 %copy-start.2 = (f32[128,8]{0,1:T(8,128)S(1)}, f32[128,8]{0,1:T(8,128)}, u32[]{:S(2)}) copy-start(f32[128,8]{0,1:T(8,128)} %param.9) | copy-start | bytes 12292
  368.8 63.5 %all-to-all-start.3 = ((bf16[16,2,40,1024]{3,2,1,0:T(8,128)(2,1)}), bf16[16,2,40,1024]{3,2,1,0:T(8,128)(2,1)}, u32[]{:S(2)}, u32[]{:S(2)}) async-start(bf16[16,2,40,1024]{3,2,1,0:T(8,128)(2,1)} %copy.30), calls=%async_computation.3 | async-start | bytes 5242880 | tf_op jit(solution)/shard_map/all_to_all | solution.py:93
Sparse Core Ops, SparseCore 0:
  134.1 51.6 reduce-scatter.4
  201.4 59.6 all-reduce.1
  266.3 31.6 all-gather.2
  299.4 53.7 all-gather.4
where the time goes:
time: 455 us; the launch traced here: 454 us
  waiting for transfers between devices  183 us (40%)
  blocking collectives  129 us (28%)
  local copies, waits for them, and re-layouts  51.8 us (11%)
  other arithmetic  39.5 us (9%)
  matrix products  25.4 us (6%)
  between operations  13.9 us (3%)
  starting transfers between devices  11.4 us (3%)
    all_to_all x1, blocking collectives, per_device(): lax.all_to_all(token_rows, 'expert', split_axis=0, concat_axis=0, tiled=T...  64.9 us
    all_to_all x1, blocking collectives, per_device(): lax.all_to_all(grad_rows_out, 'expert', split_axis=0, concat_axis=0, tile...  63.6 us
    psum x1, waiting for transfers between devices, per_device(): lax.psum(jnp.einsum('secd,efd->secf', piece, w_down, preferred_element_ty...  55.2 us
    all_to_all x1, waiting for transfers between devices, per_device(): lax.all_to_all(grad_rows, 'expert', split_axis=0, concat_axis=0, tiled=True)  50.5 us
    all_gather x1, waiting for transfers between devices, per_device(): lax.all_gather(act_grad(own_sums, own_back, hidden), 'dp', axis=0, tiled=...  43.1 us
    all_gather x1, waiting for transfers between devices, per_device(): lax.all_gather(activate(own_sums, hidden), 'dp', axis=0, tiled=True)  28.7 us
    another operation x4, other arithmetic  20.9 us
    gather x2, local copies, waits for them, and re-layouts, combine(): flat_rows[position].reshape(tok_rows, top_count, -1).astype(jnp.float32)  16.3 us
  transfers between devices with their start and end apart: 6, of which 5 were waited for; matrix products, arithmetic and copies ran while one was open for 8% of the time, Pallas kernels for 0%

commit v1 on v0

v1 whole, which is shorter than its diff:
```python
import jax
import jax.numpy as jnp
from jax import lax
from jax.sharding import PartitionSpec as P

F32 = jnp.float32
BF16 = jnp.bfloat16


def slot_maps(ids, mix, first, local_experts, capacity):
    tok_rows = ids.shape[1]
    own = first + jnp.arange(local_experts, dtype=jnp.int32)
    hit = ids[:, None, :, :] == own[None, :, None, None]
    named = jnp.any(hit, axis=3)
    weight = jnp.sum(jnp.where(hit, mix[:, None, :, :], 0.0), axis=3)
    before = jnp.arange(tok_rows)[:, None] < jnp.arange(tok_rows)[None, :]
    place = jnp.einsum(
        "set,tu->seu", named.astype(BF16), before.astype(BF16), preferred_element_type=F32
    ).astype(jnp.int32)
    slots = jnp.arange(capacity, dtype=jnp.int32)
    pick = (place[:, :, None, :] == slots[None, None, :, None]) & named[:, :, None, :]
    slot_weight = jnp.sum(jnp.where(pick, weight[:, :, None, :], 0.0), axis=3)
    return pick.astype(BF16), slot_weight


def per_device(soft_tokens, expert_ids, gate_mix, w_gate, w_up, w_down, out_grad):
    tok_rows, width_part = soft_tokens.shape
    top_count = expert_ids.shape[1]
    local_experts = w_gate.shape[0]
    hidden = w_gate.shape[2]
    groups = lax.axis_size("expert")
    dp_count = lax.axis_size("dp")
    experts = groups * local_experts
    capacity = max(2, tok_rows * top_count * 5 // (4 * experts))
    both = lax.all_gather(jnp.concatenate([soft_tokens, out_grad], axis=1), "expert")
    ids = lax.all_gather(expert_ids, "expert")
    mix = lax.all_gather(gate_mix, "expert")
    first = lax.axis_index("expert") * local_experts
    pick, slot_weight = slot_maps(ids, mix, first, local_experts, capacity)
    rows = jnp.einsum("sect,std->secd", pick, both, preferred_element_type=F32).astype(BF16)
    pre = [
        jnp.einsum("secd,edf->secf", rows[..., :width_part], w, preferred_element_type=F32)
        for w in (w_gate, w_up)
    ]
    back = jnp.einsum("secd,efd->secf", rows[..., width_part:], w_down, preferred_element_type=F32)
    part = jnp.concatenate(pre + [back], axis=-1).astype(BF16)
    total = part.astype(F32)
    moved = part
    for _ in range(dp_count - 1):
        moved = lax.ppermute(moved, "dp", [(i, (i + 1) % dp_count) for i in range(dp_count)])
        total = total + moved.astype(F32)
    a = total[..., :hidden]
    b = total[..., hidden : 2 * hidden]
    back = total[..., 2 * hidden :] * slot_weight[..., None]
    sig = jax.nn.sigmoid(a)
    act = (a * sig * b * slot_weight[..., None]).astype(BF16)
    d_gate = (back * b * sig * (1.0 + a * (1.0 - sig))).astype(BF16)
    d_up = (back * a * sig).astype(BF16)
    out = jnp.einsum("secf,efd->secd", act, w_down, preferred_element_type=F32)
    grad = jnp.einsum("secf,edf->secd", d_gate, w_gate, preferred_element_type=F32) + jnp.einsum(
        "secf,edf->secd", d_up, w_up, preferred_element_type=F32
    )
    result = jnp.concatenate([out, grad], axis=-1).astype(BF16)
    spread = jnp.einsum("sect,secd->std", pick, result, preferred_element_type=F32).astype(BF16)
    summed = lax.psum_scatter(spread, "expert", scatter_dimension=0, tiled=False)
    return summed[:, :width_part], summed[:, width_part:]


def solution(mesh):
    in_specs = (
        P("expert", "dp"),
        P("expert", None),
        P("expert", None),
        P("expert", "dp", None),
        P("expert", "dp", None),
        P("expert", None, "dp"),
        P("expert", "dp"),
    )
    out_specs = (P("expert", "dp"), P("expert", "dp"))
    return jax.shard_map(
        per_device, mesh=mesh, in_specs=in_specs, out_specs=out_specs, check_vma=False
    )
```

time: 455 us -> 362 us (0.80)
  the two profiles are of different devices: /device:TPU:11 before, /device:TPU:0 now
where the time goes in v1:
time: 362 us
  waiting for transfers between devices  264 us (73%)
  blocking collectives  43.4 us (12%)
  matrix products  23.3 us (6%)
  between operations  14.2 us (4%)
  other arithmetic  11.7 us (3%)
  local copies, waits for them, and re-layouts  3.78 us (1%)
    ppermute x1, waiting for transfers between devices, per_device(): lax.ppermute(moved, 'dp', [(i, (i + 1) % dp_count) for i in range(dp_coun...  108 us
    reduce_scatter x1, waiting for transfers between devices, per_device(): lax.psum_scatter(spread, 'expert', scatter_dimension=0, tiled=False)  102 us
    all_gather x1, waiting for transfers between devices, per_device(): lax.all_gather(jnp.concatenate([soft_tokens, out_grad], axis=1), 'expert')  53.6 us
    all_gather x1, blocking collectives, per_device(): ids = lax.all_gather(expert_ids, 'expert')  24 us
    all_gather x1, blocking collectives, per_device(): mix = lax.all_gather(gate_mix, 'expert')  19.3 us
  transfers between devices with their start and end apart: 3, of which 3 were waited for; matrix products, arithmetic and copies ran while one was open for 0% of the time, Pallas kernels for 0%

profile of v1, /device:TPU:0, one launch (start us, length us, event | category | flops | bytes accessed | tf_op | source)
XLA Modules:
  0.0 361.9 jit_solution(3081980324814529904)
XLA Ops:
  7.2 0.0 copy-start
  7.2 0.0 all-gather.5.cloned.1.call-start
  7.2 2.1 pad_maximum_fusion.1
  9.3 0.0 all-gather.5.cloned.1.call-update
  9.3 0.0 reduce-scatter.2.cloned.1.call-start
  9.4 24.0 %all-gather = s32[2048,8]{0,1:T(8,128)S(1)} all-gather(s32[128,8]{0,1:T(8,128)} %param.8), channel_id=2, replica_groups=mesh['dp'=2,'expert'=16] {'expert'}, dimensions={0}, use_global_device_ids=true | all-gather | bytes 69632 | tf_op jit(solution)/shard_map/all_gather | solution.py:36
  33.4 0.1 compare_reduce_fusion
  33.6 0.1 convolution_convert_fusion.1
  33.7 53.6 %all-gather.5.cloned.1.call-done = bf16[2048,2048]{1,0:T(8,128)(2,1)} async-done(((bf16[128,2048]{1,0:T(8,128)(2,1)}), bf16[2048,2048]{1,0:T(8,128)(2,1)}) %all-gather.5.cloned.1.call-update) | async-done | bytes 8388624 | tf_op jit(solution)/shard_map/all_gather | solution.py:35
  87.3 4.9 %convolution_convert_fusion = bf16[16,2,40,2048]{3,2,1,0:T(8,128)(2,1)S(1)} fusion(bf16[16,128,2048,1]{2,1,3,0:T(8,128)(2,1)} %bitcast.56, s32[16,2,128]{2,1,0:T(2,128)S(1)} %copy.25, pred[16,2,128]{2,1,0:T(4,128)(4,1)S(1)} %compare_reduce_fusion), kind=kOutput, calls=%fused_computation.7 | convolution fusion | flops 674037760 | bytes 13651968 | tf_op jit(solution)/shard_map/sect,std->secd/dot_general | solution.py:40
  92.2 0.0 copy-start.2
  92.2 0.8 fusion.52
  93.0 1.0 copy-done.2
  94.1 2.3 convert_bitcast_fusion.2
  96.4 2.3 convert_bitcast_fusion.3
  98.6 2.4 convert_bitcast_fusion.1
  101.0 0.0 copy-start.1
  101.0 4.9 %pad_maximum_fusion = bf16[16,2,40,2304]{3,2,0,1:T(8,128)(2,1)} fusion(bf16[16,2,40,768]{3,2,0,1:T(8,128)(2,1)S(1)} %convert_bitcast_fusion.1, bf16[16,2,40,768]{3,2,0,1:T(8,128)(2,1)S(1)} %convert_bitcast_fusion.2, bf16[16,2,40,768]{3,2,0,1:T(8,128)(2,1)S(1)} %convert_bitcast_fusion.3), kind=kLoop, calls=%fused_computation.2 | loop fusion | flops 17694720 | bytes 11796480 | tf_op jit(solution)/shard_map/concatenate | solution.py:46
  105.9 1.5 collective-permute-start
  107.3 19.3 %all-gather.2 = f32[2048,8]{0,1:T(8,128)S(1)} all-gather(f32[128,8]{0,1:T(8,128)S(1)} %copy-done.1), channel_id=4, replica_groups=mesh['dp'=2,'expert'=16] {'expert'}, dimensions={0}, use_global_device_ids=true | all-gather | bytes 69632 | tf_op jit(solution)/shard_map/all_gather | solution.py:37
  126.7 0.1 fusion.47
  126.8 0.3 select_reduce_fusion
  127.1 108.2 %collective-permute-done = bf16[16,2,40,2304]{3,2,0,1:T(8,128)(2,1)S(1)} collective-permute-done((bf16[16,2,40,2304]{3,2,0,1:T(8,128)(2,1)}, bf16[16,2,40,2304]{3,2,0,1:T(8,128)(2,1)S(1)}, u32[]{:S(2)}, u32[]{:S(2)}) %collective-permute-start) | collective-permute-done | bytes 5898272 | tf_op jit(solution)/shard_map/ppermute | solution.py:50
  235.3 1.4 convert_add_fusion
  236.7 2.9 multiply_convert_fusion.2
  239.6 2.2 convert_bitcast_fusion
  241.8 2.3 fusion.11
  244.1 2.3 fusion.15
  246.4 4.6 %bitcast_convert_fusion = bf16[16,128,2048]{2,1,0:T(8,128)(2,1)} fusion(bf16[16,2,40,1024]{3,2,1,0:T(8,128)(2,1)S(1)} %fusion.15, bf16[16,2,40,1024]{3,2,1,0:T(8,128)(2,1)S(1)} %convert_bitcast_fusion, s32[16,2,128]{2,1,0:T(2,128)S(1)} %copy.25, pred[16,2,128]{2,1,0:T(4,128)(4,1)S(1)} %compare_reduce_fusion), kind=kOutput, calls=%fused_computation | convolution fusion | flops 686096384 | bytes 13651968 | tf_op jit(solution)/shard_map/sect,secd->std/dot_general | solution.py:64
  251.0 0.0 reduce-scatter.2.cloned.1.call-update
  251.0 102.2 %reduce-scatter.2.cloned.1.call-done = bf16[1,128,2048]{2,1,0:T(8,128)(2,1)} async-done(((bf16[16,128,2048]{2,1,0:T(8,128)(2,1)}), bf16[1,128,2048]{2,1,0:T(8,128)(2,1)}) %reduce-scatter.2.cloned.1.call-update) | async-done | bytes 524304 | tf_op jit(solution)/shard_map/reduce_scatter | solution.py:65
  353.2 1.9 fusion.53
  (11 shorter events, 0.0 us)
Async XLA Ops:
  7.2 91.5 %copy-start = (bf16[2,768,1024]{2,1,0:T(8,128)(2,1)S(1)}, bf16[2,768,1024]{2,1,0:T(8,128)(2,1)}, u32[]{:S(2)}) copy-start(bf16[2,768,1024]{2,1,0:T(8,128)(2,1)} %param.12) | copy-start | bytes 9437188
  7.2 80.1 %all-gather.5.cloned.1.call-start = ((), (), s32[]{:S(2)}) async-start(), calls=%async_computation.2 | async-start | bytes 8912896 | tf_op jit(solution)/shard_map/all_gather | solution.py:35
  9.3 343.9 %reduce-scatter.2.cloned.1.call-start = ((), (), s32[]{:S(2)}) async-start(), calls=%async_computation.1 | async-start | bytes 8912896 | tf_op jit(solution)/shard_map/reduce_scatter | solution.py:65
  92.2 1.9 copy-start.2
  94.1 2.3 copy-start.4
  101.0 6.3 %copy-start.1 = (f32[128,8]{0,1:T(8,128)S(1)}, f32[128,8]{0,1:T(8,128)}, u32[]{:S(2)}) copy-start(f32[128,8]{0,1:T(8,128)} %param.9) | copy-start | bytes 12292
  105.9 129.4 %collective-permute-start = (bf16[16,2,40,2304]{3,2,0,1:T(8,128)(2,1)}, bf16[16,2,40,2304]{3,2,0,1:T(8,128)(2,1)S(1)}, u32[]{:S(2)}, u32[]{:S(2)}) collective-permute-start(bf16[16,2,40,2304]{3,2,0,1:T(8,128)(2,1)} %pad_maximum_fusion), channel_id=1, source_target_pairs={{0,16},{16,0},{1,17},{17,1},{2,18},{18,2},{3,19},{19,3},{4,20},{20... | collective-permute-start | bytes 17694728 | tf_op jit(solution)/shard_map/ppermute | solution.py:50
  239.6 2.2 copy-start.3
  241.8 2.3 copy-start.5
Sparse Core Ops, SparseCore 0:
  10.1 77.0 all-gather.4
  251.1 102.0 reduce-scatter.1

commit v2 on v1

--- a/solution.py
+++ b/solution.py
@@ -1,6 +1,10 @@
+import functools
+
 import jax
 import jax.numpy as jnp
 from jax import lax
+from jax.experimental import pallas as pl
+from jax.experimental.pallas import tpu as pltpu
 from jax.sharding import PartitionSpec as P
 
 F32 = jnp.float32
@@ -66,6 +70,301 @@
     return summed[:, :width_part], summed[:, width_part:]
 
 
+MESH = pl.DeviceIdType.MESH
+MID = 2
+CORES = 2
+
+
+def flip(value, step, count):
+    out, bit = 0, 1
+    while bit < count:
+        out = out + lax.rem(lax.div(value, bit) + lax.div(step, bit), 2) * bit
+        bit *= 2
+    return out
+
+
+def fused_kernel(
+    groups, x_ref, meta_ref, wg_ref, wu_ref, wd_ref, mixed_ref, tgrad_ref,
+    ag, metas, psend, precv, acc, crecv, xsend, xrecv, zsend, zrecv,
+    ms, mr, zs, zr, xs, xr, cs, cr, ys, yr, rcs, rcr, rxs, rxr, rzs, rzr,
+):
+    rows, wide = x_ref.shape
+    half = wide // 2
+    experts, _, hid = wg_ref.shape
+    plane = MID * CORES
+    outer = groups // plane
+    slots = psend.shape[1] // experts
+    me = lax.axis_index("expert")
+    y = lax.axis_index("dp")
+    z = lax.div(me, plane)
+    x = lax.rem(lax.div(me, CORES), MID)
+    c = lax.rem(me, CORES)
+    core_peer = (z * MID + x) * CORES + 1 - c
+    x_peer = (z * MID + 1 - x) * CORES + c
+
+    def at(expert):
+        return {"dp": y, "expert": expert}
+
+    def copy(src, dst, send, recv, device):
+        return pltpu.make_async_remote_copy(
+            src_ref=src, dst_ref=dst, send_sem=send, recv_sem=recv,
+            device_id=device, device_id_type=MESH,
+        )
+
+    barrier = pltpu.get_barrier_semaphore()
+    for k in range(1, groups):
+        pl.semaphore_signal(
+            barrier, inc=1, device_id=at(lax.rem(me + k, groups)), device_id_type=MESH
+        )
+    other_dp = {"dp": 1 - y, "expert": me}
+    pl.semaphore_signal(barrier, inc=1, device_id=other_dp, device_id_type=MESH)
+    pl.semaphore_wait(barrier, groups)
+
+    def meta_copy(k):
+        to = lax.rem(me + k, groups)
+        return copy(meta_ref.at[to], metas.at[me], ms.at[k], mr.at[k], at(to))
+
+    def meta_arrival(k):
+        source = lax.rem(me + groups - k, groups)
+        return copy(meta_ref.at[source], metas.at[source], ms.at[k], mr.at[k], at(source))
+
+    def peer_of(step):
+        return (flip(z, step, outer) * MID + x) * CORES + c
+
+    def z_copy(step):
+        return copy(x_ref, ag.at[me], zs.at[step], zr.at[step], at(peer_of(step)))
+
+    def z_arrival(step):
+        blk = peer_of(step)
+        return copy(x_ref, ag.at[blk], zs.at[step], zr.at[step], at(blk))
+
+    def x_copy(step, blk):
+        return copy(ag.at[blk], ag.at[blk], xs.at[step], xr.at[step], at(x_peer))
+
+    def c_copy(step, which, blk):
+        return copy(
+            ag.at[blk], ag.at[blk], cs.at[step, which], cr.at[step, which], at(core_peer)
+        )
+
+    def y_copy(step):
+        return copy(psend.at[step], precv.at[step], ys.at[step], yr.at[step], other_dp)
+
+    def rc_copy(step, across):
+        return copy(
+            acc.at[across * CORES + 1 - c], crecv.at[step, across],
+            rcs.at[step, across], rcr.at[step, across], at(core_peer),
+        )
+
+    def rx_copy(step):
+        return copy(xsend, xrecv.at[step], rxs.at[step], rxr.at[step], at(x_peer))
+
+    def rz_copy(step):
+        return copy(zsend.at[step], zrecv.at[step], rzs.at[step], rzr.at[step], at(peer_of(step)))
+
+    ag[me] = x_ref[...]
+    metas[me] = meta_ref[me]
+    for k in range(1, groups):
+        meta_copy(k).start()
+    for i in range(1, outer):
+        z_copy(outer - i).start()
+
+    def dot(a, b, dims):
+        return lax.dot_general(a, b, (dims, ((), ())), preferred_element_type=jnp.float32)
+
+    def pick_of(p):
+        tiles = metas[pl.ds(p * plane, plane)]
+        line = jnp.concatenate([tiles[b] for b in range(plane)], axis=1)
+        slot = lax.broadcasted_iota(jnp.int32, (slots, plane * rows), 0).astype(jnp.float32)
+        picks, weights = [], []
+        for e in range(experts):
+            match = slot == line[e : e + 1]
+            picks.append(jnp.where(match, 1.0, 0.0))
+            weights.append(
+                jnp.sum(
+                    jnp.where(match, line[experts + e : experts + e + 1], 0.0),
+                    axis=1, keepdims=True,
+                )
+            )
+        return jnp.concatenate(picks, axis=0), weights
+
+    def first_half(i):
+        step = lax.rem(outer - i, outer)
+        p = flip(z, step, outer)
+        mine = (p * MID + x) * CORES + c
+        across = (p * MID + 1 - x) * CORES + c
+
+        @pl.when(i > 0)
+        def _():
+            z_arrival(step).wait_recv()
+
+        x_copy(step, mine).start()
+        c_copy(step, 0, mine).start()
+
+        @pl.when(i == 0)
+        def _():
+            @pl.loop(1, groups)
+            def _(k):
+                meta_arrival(k).wait_recv()
+
+        x_copy(step, across).wait_recv()
+        c_copy(step, 1, across).start()
+        c_copy(step, 0, mine + 1 - 2 * c).wait_recv()
+        c_copy(step, 1, across + 1 - 2 * c).wait_recv()
+        pick, _ = pick_of(p)
+        pick = pick.astype(BF16)
+        block = ag[pl.ds(p * plane, plane)].reshape(plane * rows, wide)
+        got = dot(pick, block, ((1,), (0,))).astype(BF16)
+        for e in range(experts):
+            tok = got[e * slots : (e + 1) * slots, :half]
+            cot = got[e * slots : (e + 1) * slots, half:]
+            span = pl.ds(e * slots, slots)
+            psend[step, span, :hid] = dot(tok, wg_ref[e], ((1,), (0,))).astype(BF16)
+            psend[step, span, hid : 2 * hid] = dot(tok, wu_ref[e], ((1,), (0,))).astype(BF16)
+            psend[step, span, 2 * hid :] = dot(cot, wd_ref[e], ((1,), (1,))).astype(BF16)
+        y_copy(step).start()
+
+    def second_half(i):
+        step = lax.rem(outer - i, outer)
+        p = flip(z, step, outer)
+        pick, weights = pick_of(p)
+        spread_by = pick.T.astype(BF16)
+        y_copy(step).wait_recv()
+        outs, grads = [], []
+        for e in range(experts):
+            span = pl.ds(e * slots, slots)
+
+            def total(lo):
+                part = psend[step, span, lo : lo + hid].astype(F32)
+                return part + precv[step, span, lo : lo + hid].astype(F32)
+
+            a, b = total(0), total(hid)
+            back = total(2 * hid) * weights[e]
+            sig = jax.nn.sigmoid(a)
+            silu = a * sig
+            act = (silu * b * weights[e]).astype(BF16)
+            d_gate = (back * b * sig * (1.0 + a * (1.0 - sig))).astype(BF16)
+            d_up = (back * silu).astype(BF16)
+            outs.append(dot(act, wd_ref[e], ((1,), (0,))).astype(BF16))
+            grads.append(
+                (
+                    dot(d_gate, wg_ref[e], ((1,), (1,))) + dot(d_up, wu_ref[e], ((1,), (1,)))
+                ).astype(BF16)
+            )
+        for lo, part in ((0, outs), (half, grads)):
+            rows_out = dot(spread_by, jnp.concatenate(part, axis=0), ((1,), (0,)))
+            acc[:, :, lo : lo + half] = rows_out.astype(BF16).reshape(plane, rows, half)
+        for m in range(MID):
+            rc_copy(step, m).start()
+        for m in range(MID):
+            rc_copy(step, m).wait_recv()
+        there = acc[(1 - x) * CORES + c].astype(F32) + crecv[step, 1 - x].astype(F32)
+        xsend[...] = there.astype(BF16)
+        rx_copy(step).start()
+        here = acc[x * CORES + c].astype(F32) + crecv[step, x].astype(F32)
+        rx_copy(step).wait_recv()
+        here = (here + xrecv[step].astype(F32)).astype(BF16)
+
+        @pl.when(i == 0)
+        def _():
+            zrecv[0] = here
+
+        @pl.when(i > 0)
+        def _():
+            zsend[step] = here
+            rz_copy(step).start()
+
+        rx_copy(step).wait_send()
+        for m in range(MID):
+            rc_copy(step, m).wait_send()
+
+    @pl.loop(0, outer + 1)
+    def _(i):
+        @pl.when(i < outer)
+        def _():
+            first_half(i)
+
+        @pl.when(i > 0)
+        def _():
+            second_half(i - 1)
+
+    @pl.loop(1, groups)
+    def _(k):
+        meta_copy(k).wait_send()
+
+    for step in range(outer):
+        x_copy(step, me).wait_send()
+        c_copy(step, 0, me).wait_send()
+        c_copy(step, 1, me).wait_send()
+        y_copy(step).wait_send()
+    for step in range(1, outer):
+        z_copy(step).wait_send()
+    final = zrecv[0].astype(F32)
+    for step in range(1, outer):
+        rz_copy(step).wait_recv()
+        final = final + zrecv[step].astype(F32)
+    for step in range(1, outer):
+        rz_copy(step).wait_send()
+    mixed_ref[...] = final[:, :half].astype(BF16)
+    tgrad_ref[...] = final[:, half:].astype(BF16)
+
+
+def fused_device(soft_tokens, expert_ids, gate_mix, w_gate, w_up, w_down, out_grad):
+    tok_rows, width_part = soft_tokens.shape
+    top_count = expert_ids.shape[1]
+    local_experts, _, hid = w_gate.shape
+    groups = lax.axis_size("expert")
+    experts = groups * local_experts
+    capacity = max(2, tok_rows * top_count * 5 // (4 * experts))
+    plane = MID * CORES
+    outer = groups // plane
+    wide = 2 * width_part
+    ids, mix = expert_ids.T, gate_mix.T
+    hit = ids[None] == jnp.arange(experts, dtype=jnp.int32)[:, None, None]
+    named = jnp.any(hit, axis=1)
+    weight = jnp.sum(jnp.where(hit, mix[None], 0.0), axis=1)
+    before = jnp.arange(tok_rows)[:, None] < jnp.arange(tok_rows)[None, :]
+    place = jnp.dot(named.astype(BF16), before.astype(BF16), preferred_element_type=F32)
+    offset = (lax.axis_index("expert") % plane * capacity).astype(F32)
+    key = jnp.where(named, place + offset, -1.0)
+    shape = (groups, local_experts, tok_rows)
+    meta = jnp.concatenate([key.reshape(shape), weight.reshape(shape)], axis=1)
+    meta = jnp.pad(meta, ((0, 0), (0, -2 * local_experts % 8), (0, 0)))
+    both = jnp.concatenate([soft_tokens, out_grad], axis=1)
+    picked = local_experts * plane * capacity
+    vmem = pl.BlockSpec(memory_space=pltpu.VMEM)
+    dma = pltpu.SemaphoreType.DMA
+    out = jax.ShapeDtypeStruct((tok_rows, width_part), BF16)
+    return pl.pallas_call(
+        functools.partial(fused_kernel, groups),
+        out_shape=(out, out),
+        in_specs=[vmem] * 5,
+        out_specs=(vmem, vmem),
+        scratch_shapes=[
+            pltpu.VMEM((groups, tok_rows, wide), BF16),
+            pltpu.VMEM(meta.shape, F32),
+            pltpu.VMEM((outer, picked, 3 * hid), BF16),
+            pltpu.VMEM((outer, picked, 3 * hid), BF16),
+            pltpu.VMEM((plane, tok_rows, wide), BF16),
+            pltpu.VMEM((outer, MID, tok_rows, wide), BF16),
+            pltpu.VMEM((tok_rows, wide), BF16),
+            pltpu.VMEM((outer, tok_rows, wide), BF16),
+            pltpu.VMEM((outer, tok_rows, wide), BF16),
+            pltpu.VMEM((outer, tok_rows, wide), BF16),
+            dma((groups,)), dma((groups,)),
+            dma((outer,)), dma((outer,)),
+            dma((outer,)), dma((outer,)),
+            dma((outer, MID)), dma((outer, MID)),
+            dma((outer,)), dma((outer,)),
+            dma((outer, MID)), dma((outer, MID)),
+            dma((outer,)), dma((outer,)),
+            dma((outer,)), dma((outer,)),
+        ],
+        compiler_params=pltpu.CompilerParams(
+            collective_id=0, has_side_effects=True, vmem_limit_bytes=67043328
+        ),
+    )(both, meta, w_gate, w_up, w_down)
+
+
 def solution(mesh):
     in_specs = (
         P("expert", "dp"),
@@ -77,6 +376,8 @@
         P("expert", "dp"),
     )
     out_specs = (P("expert", "dp"), P("expert", "dp"))
+    fits = mesh.shape["dp"] == 2 and mesh.shape["expert"] in (4, 8, 16)
     return jax.shard_map(
-        per_device, mesh=mesh, in_specs=in_specs, out_specs=out_specs, check_vma=False
+        fused_device if fits else per_device,
+        mesh=mesh, in_specs=in_specs, out_specs=out_specs, check_vma=False,
     )

time: 362 us -> 223 us (0.62)
  waiting for transfers between devices: 264 us -> 0 us
  Pallas kernels: 0 us -> 215 us
  blocking collectives: 43.4 us -> 0 us
  matrix products: 23.3 us -> 0.14 us
  between operations: 14.2 us -> 0.66 us
  other arithmetic: 11.7 us -> 4 us
    pallas_call x0 -> x1, Pallas kernels: none -> 215 us  [fused_device(): pl.pallas_call(functools.partial(fused_kernel, groups), out_shape=(out, o...]
    ppermute x1 -> x0, waiting for transfers between devices: 108 us -> none  [per_device(): lax.ppermute(moved, 'dp', [(i, (i + 1) % dp_count) for i in range(dp_coun...]
    reduce_scatter x1 -> x0, waiting for transfers between devices: 102 us -> none  [per_device(): lax.psum_scatter(spread, 'expert', scatter_dimension=0, tiled=False)]
    all_gather x1 -> x0, waiting for transfers between devices: 53.6 us -> none  [per_device(): lax.all_gather(jnp.concatenate([soft_tokens, out_grad], axis=1), 'expert')]
    all_gather x2 -> x0, blocking collectives: 43.4 us -> none  [the longest x1 24 us: per_device(): ids = lax.all_gather(expert_ids, 'expert')]
    dot_general x9 -> x1, matrix products: 23.3 us -> 0.14 us  [fused_device(): jnp.dot(named.astype(BF16), before.astype(BF16), preferred_element_type=F32)]
    concatenate x2, other arithmetic: 6.93 us -> 2.51 us  [the longest x1 1.86 us: fused_device(): both = jnp.concatenate([soft_tokens, out_grad], axis=1)]
  transfers between devices with their start and end apart: 3 -> 0, of which waited for: 3 -> 0; matrix products, arithmetic and copies ran while one was open for 0% -> 0% of each run, Pallas kernels for 0% -> 0%
where the time goes in v2:
time: 223 us
  Pallas kernels  215 us (96%)
  other arithmetic  4 us (2%)
  local copies, waits for them, and re-layouts  3.34 us (1%)
    pallas_call x1, Pallas kernels, fused_device(): pl.pallas_call(functools.partial(fused_kernel, groups), out_shape=(out, o...  215 us

profile of v2, /device:TPU:0, one launch (start us, length us, event | category | flops | bytes accessed | tf_op | source)
XLA Modules:
  0.0 222.9 jit_solution(15855294801254315868)
XLA Ops:
  0.6 0.7 fusion.1
  1.4 0.1 fusion
  1.5 0.8 select_reduce_fusion
  2.3 0.7 select_maximum_fusion.meta_ref
  2.9 1.9 pad_maximum_fusion.x_ref
  4.8 214.8 %shard_map.86 = (bf16[128,1024]{1,0:T(8,128)(2,1)}, bf16[128,1024]{1,0:T(8,128)(2,1)}) custom-call(bf16[128,2048]{1,0:T(8,128)(2,1)} %pad_maximum_fusion.x_ref, f32[16,8,128]{2,1,0:T(8,128)} %select_maximum_fusion.meta_ref, bf16[2,1024,768]{2,1,0:T(8,128)(2,1)} %wg_ref.1, bf16[2,1024,768]{2,1,0:T(8,128)(2,1)} %wu_ref.1, bf16[2,768,1024]{2,1,0:T(8,128)(2,1)} %wd_ref.1), custom_call_target="tpu_custom_call" | custom-call | tf_op jit(solution)/shard_map/pallas_call | solution.py:337
  219.5 1.7 copy.11
  221.2 1.7 copy.12

commit v3 on v2

--- a/solution.py
+++ b/solution.py
@@ -93,7 +93,7 @@
     experts, _, hid = wg_ref.shape
     plane = MID * CORES
     outer = groups // plane
-    slots = psend.shape[1] // experts
+    slots = psend.shape[2]
     me = lax.axis_index("expert")
     y = lax.axis_index("dp")
     z = lax.div(me, plane)
@@ -146,20 +146,28 @@
             ag.at[blk], ag.at[blk], cs.at[step, which], cr.at[step, which], at(core_peer)
         )
 
-    def y_copy(step):
-        return copy(psend.at[step], precv.at[step], ys.at[step], yr.at[step], other_dp)
-
-    def rc_copy(step, across):
+    def y_copy(step, e):
         return copy(
-            acc.at[across * CORES + 1 - c], crecv.at[step, across],
-            rcs.at[step, across], rcr.at[step, across], at(core_peer),
-        )
-
-    def rx_copy(step):
-        return copy(xsend, xrecv.at[step], rxs.at[step], rxr.at[step], at(x_peer))
-
-    def rz_copy(step):
-        return copy(zsend.at[step], zrecv.at[step], rzs.at[step], rzr.at[step], at(peer_of(step)))
+            psend.at[step, e], precv.at[step, e], ys.at[step, e], yr.at[step, e], other_dp
+        )
+
+    def rc_copy(step, part, across):
+        return copy(
+            acc.at[part, across * CORES + 1 - c], crecv.at[step, part, across],
+            rcs.at[step, part, across], rcr.at[step, part, across], at(core_peer),
+        )
+
+    def rx_copy(step, part):
+        return copy(
+            xsend.at[part], xrecv.at[step, part],
+            rxs.at[step, part], rxr.at[step, part], at(x_peer),
+        )
+
+    def rz_copy(step, part):
+        return copy(
+            zsend.at[step, part], zrecv.at[step, part],
+            rzs.at[step, part], rzr.at[step, part], at(peer_of(step)),
+        )
 
     ag[me] = x_ref[...]
     metas[me] = meta_ref[me]
@@ -213,29 +221,26 @@
         pick, _ = pick_of(p)
         pick = pick.astype(BF16)
         block = ag[pl.ds(p * plane, plane)].reshape(plane * rows, wide)
-        got = dot(pick, block, ((1,), (0,))).astype(BF16)
         for e in range(experts):
-            tok = got[e * slots : (e + 1) * slots, :half]
-            cot = got[e * slots : (e + 1) * slots, half:]
-            span = pl.ds(e * slots, slots)
-            psend[step, span, :hid] = dot(tok, wg_ref[e], ((1,), (0,))).astype(BF16)
-            psend[step, span, hid : 2 * hid] = dot(tok, wu_ref[e], ((1,), (0,))).astype(BF16)
-            psend[step, span, 2 * hid :] = dot(cot, wd_ref[e], ((1,), (1,))).astype(BF16)
-        y_copy(step).start()
+            got = dot(pick[e * slots : (e + 1) * slots], block, ((1,), (0,))).astype(BF16)
+            tok, cot = got[:, :half], got[:, half:]
+            psend[step, e, :, :hid] = dot(tok, wg_ref[e], ((1,), (0,))).astype(BF16)
+            psend[step, e, :, hid : 2 * hid] = dot(tok, wu_ref[e], ((1,), (0,))).astype(BF16)
+            psend[step, e, :, 2 * hid :] = dot(cot, wd_ref[e], ((1,), (1,))).astype(BF16)
+            y_copy(step, e).start()
 
     def second_half(i):
         step = lax.rem(outer - i, outer)
         p = flip(z, step, outer)
         pick, weights = pick_of(p)
         spread_by = pick.T.astype(BF16)
-        y_copy(step).wait_recv()
-        outs, grads = [], []
+        outs, changes = [], []
         for e in range(experts):
-            span = pl.ds(e * slots, slots)
+            y_copy(step, e).wait_recv()
 
             def total(lo):
-                part = psend[step, span, lo : lo + hid].astype(F32)
-                return part + precv[step, span, lo : lo + hid].astype(F32)
+                part = psend[step, e, :, lo : lo + hid].astype(F32)
+                return part + precv[step, e, :, lo : lo + hid].astype(F32)
 
             a, b = total(0), total(hid)
             back = total(2 * hid) * weights[e]
@@ -243,49 +248,66 @@
             silu = a * sig
             act = (silu * b * weights[e]).astype(BF16)
             d_gate = (back * b * sig * (1.0 + a * (1.0 - sig))).astype(BF16)
-            d_up = (back * silu).astype(BF16)
+            changes.append((d_gate, (back * silu).astype(BF16)))
             outs.append(dot(act, wd_ref[e], ((1,), (0,))).astype(BF16))
-            grads.append(
-                (
-                    dot(d_gate, wg_ref[e], ((1,), (1,))) + dot(d_up, wu_ref[e], ((1,), (1,)))
-                ).astype(BF16)
-            )
-        for lo, part in ((0, outs), (half, grads)):
-            rows_out = dot(spread_by, jnp.concatenate(part, axis=0), ((1,), (0,)))
-            acc[:, :, lo : lo + half] = rows_out.astype(BF16).reshape(plane, rows, half)
-        for m in range(MID):
-            rc_copy(step, m).start()
-        for m in range(MID):
-            rc_copy(step, m).wait_recv()
-        there = acc[(1 - x) * CORES + c].astype(F32) + crecv[step, 1 - x].astype(F32)
-        xsend[...] = there.astype(BF16)
-        rx_copy(step).start()
-        here = acc[x * CORES + c].astype(F32) + crecv[step, x].astype(F32)
-        rx_copy(step).wait_recv()
-        here = (here + xrecv[step].astype(F32)).astype(BF16)
-
-        @pl.when(i == 0)
-        def _():
-            zrecv[0] = here
-
-        @pl.when(i > 0)
-        def _():
-            zsend[step] = here
-            rz_copy(step).start()
-
-        rx_copy(step).wait_send()
-        for m in range(MID):
-            rc_copy(step, m).wait_send()
-
-    @pl.loop(0, outer + 1)
+
+        def scatter(part, values):
+            rows_out = dot(spread_by, jnp.concatenate(values, axis=0), ((1,), (0,)))
+            acc[part] = rows_out.astype(BF16).reshape(plane, rows, half)
+            for m in range(MID):
+                rc_copy(step, part, m).start()
+
+        scatter(0, outs)
+        grads = [
+            (
+                dot(changes[e][0], wg_ref[e], ((1,), (1,)))
+                + dot(changes[e][1], wu_ref[e], ((1,), (1,)))
+            ).astype(BF16)
+            for e in range(experts)
+        ]
+
+        def to_x_peer(part):
+            for m in range(MID):
+                rc_copy(step, part, m).wait_recv()
+            there = acc[part, (1 - x) * CORES + c].astype(F32)
+            xsend[part] = (there + crecv[step, part, 1 - x].astype(F32)).astype(BF16)
+            rx_copy(step, part).start()
+
+        def to_owner(part):
+            here = acc[part, x * CORES + c].astype(F32) + crecv[step, part, x].astype(F32)
+            rx_copy(step, part).wait_recv()
+            here = (here + xrecv[step, part].astype(F32)).astype(BF16)
+
+            @pl.when(i == 0)
+            def _():
+                zrecv[0, part] = here
+
+            @pl.when(i > 0)
+            def _():
+                zsend[step, part] = here
+                rz_copy(step, part).start()
+
+        to_x_peer(0)
+        scatter(1, grads)
+        to_x_peer(1)
+        to_owner(0)
+        to_owner(1)
+        for part in range(2):
+            rx_copy(step, part).wait_send()
+            for m in range(MID):
+                rc_copy(step, part, m).wait_send()
+
+    ahead = 2
+
+    @pl.loop(0, outer + ahead)
     def _(i):
         @pl.when(i < outer)
         def _():
             first_half(i)
 
-        @pl.when(i > 0)
+        @pl.when(i >= ahead)
         def _():
-            second_half(i - 1)
+            second_half(i - ahead)
 
     @pl.loop(1, groups)
     def _(k):
@@ -295,17 +317,19 @@
         x_copy(step, me).wait_send()
         c_copy(step, 0, me).wait_send()
         c_copy(step, 1, me).wait_send()
-        y_copy(step).wait_send()
+        for e in range(experts):
+            y_copy(step, e).wait_send()
     for step in range(1, outer):
         z_copy(step).wait_send()
-    final = zrecv[0].astype(F32)
+    for part, out_ref in enumerate((mixed_ref, tgrad_ref)):
+        final = zrecv[0, part].astype(F32)
+        for step in range(1, outer):
+            rz_copy(step, part).wait_recv()
+            final = final + zrecv[step, part].astype(F32)
+        out_ref[...] = final.astype(BF16)
     for step in range(1, outer):
-        rz_copy(step).wait_recv()
-        final = final + zrecv[step].astype(F32)
-    for step in range(1, outer):
-        rz_copy(step).wait_send()
-    mixed_ref[...] = final[:, :half].astype(BF16)
-    tgrad_ref[...] = final[:, half:].astype(BF16)
+        for part in range(2):
+            rz_copy(step, part).wait_send()
 
 
 def fused_device(soft_tokens, expert_ids, gate_mix, w_gate, w_up, w_down, out_grad):
@@ -330,7 +354,7 @@
     meta = jnp.concatenate([key.reshape(shape), weight.reshape(shape)], axis=1)
     meta = jnp.pad(meta, ((0, 0), (0, -2 * local_experts % 8), (0, 0)))
     both = jnp.concatenate([soft_tokens, out_grad], axis=1)
-    picked = local_experts * plane * capacity
+    slots = plane * capacity
     vmem = pl.BlockSpec(memory_space=pltpu.VMEM)
     dma = pltpu.SemaphoreType.DMA
     out = jax.ShapeDtypeStruct((tok_rows, width_part), BF16)
@@ -342,22 +366,22 @@
         scratch_shapes=[
             pltpu.VMEM((groups, tok_rows, wide), BF16),
             pltpu.VMEM(meta.shape, F32),
-            pltpu.VMEM((outer, picked, 3 * hid), BF16),
-            pltpu.VMEM((outer, picked, 3 * hid), BF16),
-            pltpu.VMEM((plane, tok_rows, wide), BF16),
-            pltpu.VMEM((outer, MID, tok_rows, wide), BF16),
-            pltpu.VMEM((tok_rows, wide), BF16),
-            pltpu.VMEM((outer, tok_rows, wide), BF16),
-            pltpu.VMEM((outer, tok_rows, wide), BF16),
-            pltpu.VMEM((outer, tok_rows, wide), BF16),
+            pltpu.VMEM((outer, local_experts, slots, 3 * hid), BF16),
+            pltpu.VMEM((outer, local_experts, slots, 3 * hid), BF16),
+            pltpu.VMEM((2, plane, tok_rows, width_part), BF16),
+            pltpu.VMEM((outer, 2, MID, tok_rows, width_part), BF16),
+            pltpu.VMEM((2, tok_rows, width_part), BF16),
+            pltpu.VMEM((outer, 2, tok_rows, width_part), BF16),
+            pltpu.VMEM((outer, 2, tok_rows, width_part), BF16),
+            pltpu.VMEM((outer, 2, tok_rows, width_part), BF16),
             dma((groups,)), dma((groups,)),
             dma((outer,)), dma((outer,)),
             dma((outer,)), dma((outer,)),
             dma((outer, MID)), dma((outer, MID)),
-            dma((outer,)), dma((outer,)),
-            dma((outer, MID)), dma((outer, MID)),
-            dma((outer,)), dma((outer,)),
-            dma((outer,)), dma((outer,)),
+            dma((outer, local_experts)), dma((outer, local_experts)),
+            dma((outer, 2, MID)), dma((outer, 2, MID)),
+            dma((outer, 2)), dma((outer, 2)),
+            dma((outer, 2)), dma((outer, 2)),
         ],
         compiler_params=pltpu.CompilerParams(
             collective_id=0, has_side_effects=True, vmem_limit_bytes=67043328

time: 223 us -> 202 us (0.906)
  Pallas kernels: 215 us -> 193 us
    pallas_call x1, Pallas kernels: 215 us -> 193 us  [fused_device(): pl.pallas_call(functools.partial(fused_kernel, groups), out_shape=(out, o...]
where the time goes in v3:
time: 202 us; the launch traced here: 201 us
  Pallas kernels  193 us (96%)
  other arithmetic  4 us (2%)
  local copies, waits for them, and re-layouts  3.34 us (2%)
    pallas_call x1, Pallas kernels, fused_device(): pl.pallas_call(functools.partial(fused_kernel, groups), out_shape=(out, o...  193 us

profile of v3, /device:TPU:0, one launch (start us, length us, event | category | flops | bytes accessed | tf_op | source)
XLA Modules:
  0.0 201.3 jit_solution(14561121773162562701)
XLA Ops:
  0.6 0.7 fusion.1
  1.4 0.1 fusion
  1.5 0.8 select_reduce_fusion
  2.3 0.7 select_maximum_fusion.meta_ref
  2.9 1.9 pad_maximum_fusion.x_ref
  4.8 193.2 %shard_map.86 = (bf16[128,1024]{1,0:T(8,128)(2,1)}, bf16[128,1024]{1,0:T(8,128)(2,1)}) custom-call(bf16[128,2048]{1,0:T(8,128)(2,1)} %pad_maximum_fusion.x_ref, f32[16,8,128]{2,1,0:T(8,128)} %select_maximum_fusion.meta_ref, bf16[2,1024,768]{2,1,0:T(8,128)(2,1)} %wg_ref.1, bf16[2,1024,768]{2,1,0:T(8,128)(2,1)} %wu_ref.1, bf16[2,768,1024]{2,1,0:T(8,128)(2,1)} %wd_ref.1), custom_call_target="tpu_custom_call" | custom-call | tf_op jit(solution)/shard_map/pallas_call | solution.py:361
  198.0 1.7 copy.11
  199.7 1.7 copy.12

commit v4 on v3

--- a/solution.py
+++ b/solution.py
@@ -234,7 +234,12 @@
         p = flip(z, step, outer)
         pick, weights = pick_of(p)
         spread_by = pick.T.astype(BF16)
-        outs, changes = [], []
+        outs, changes, grads = [], [], []
+
+        def grad_of(e):
+            by_gate = dot(changes[e][0], wg_ref[e], ((1,), (1,)))
+            return (by_gate + dot(changes[e][1], wu_ref[e], ((1,), (1,)))).astype(BF16)
+
         for e in range(experts):
             y_copy(step, e).wait_recv()
 
@@ -250,6 +255,8 @@
             d_gate = (back * b * sig * (1.0 + a * (1.0 - sig))).astype(BF16)
             changes.append((d_gate, (back * silu).astype(BF16)))
             outs.append(dot(act, wd_ref[e], ((1,), (0,))).astype(BF16))
+            if e < experts - 1:
+                grads.append(grad_of(e))
 
         def scatter(part, values):
             rows_out = dot(spread_by, jnp.concatenate(values, axis=0), ((1,), (0,)))
@@ -258,13 +265,7 @@
                 rc_copy(step, part, m).start()
 
         scatter(0, outs)
-        grads = [
-            (
-                dot(changes[e][0], wg_ref[e], ((1,), (1,)))
-                + dot(changes[e][1], wu_ref[e], ((1,), (1,)))
-            ).astype(BF16)
-            for e in range(experts)
-        ]
+        grads.append(grad_of(experts - 1))
 
         def to_x_peer(part):
             for m in range(MID):
@@ -297,7 +298,7 @@
             for m in range(MID):
                 rc_copy(step, part, m).wait_send()
 
-    ahead = 2
+    ahead = max(1, outer - 1)
 
     @pl.loop(0, outer + ahead)
     def _(i):

time: 202 us -> 202 us (level)
  no operation moved by 1% of the time
where the time goes in v4:
time: 202 us
  Pallas kernels  194 us (96%)
  other arithmetic  4 us (2%)
  local copies, waits for them, and re-layouts  3.34 us (2%)
    pallas_call x1, Pallas kernels, fused_device(): pl.pallas_call(functools.partial(fused_kernel, groups), out_shape=(out, o...  194 us

profile of v4, /device:TPU:0, one launch (start us, length us, event | category | flops | bytes accessed | tf_op | source)
XLA Modules:
  0.0 202.1 jit_solution(11562071934817618540)
XLA Ops:
  0.6 0.7 fusion.1
  1.4 0.1 fusion
  1.5 0.8 select_reduce_fusion
  2.3 0.7 select_maximum_fusion.meta_ref
  2.9 1.9 pad_maximum_fusion.x_ref
  4.8 194.0 %shard_map.86 = (bf16[128,1024]{1,0:T(8,128)(2,1)}, bf16[128,1024]{1,0:T(8,128)(2,1)}) custom-call(bf16[128,2048]{1,0:T(8,128)(2,1)} %pad_maximum_fusion.x_ref, f32[16,8,128]{2,1,0:T(8,128)} %select_maximum_fusion.meta_ref, bf16[2,1024,768]{2,1,0:T(8,128)(2,1)} %wg_ref.1, bf16[2,1024,768]{2,1,0:T(8,128)(2,1)} %wu_ref.1, bf16[2,768,1024]{2,1,0:T(8,128)(2,1)} %wd_ref.1), custom_call_target="tpu_custom_call" | custom-call | tf_op jit(solution)/shard_map/pallas_call | solution.py:362
  198.8 1.7 copy.11
  200.4 1.7 copy.12
